TPU v7x, 32 devices: a whole 2x2x4 slice. The times are simulated.
32 devices in a mesh: gx: 4 (over x, core), gy: 8 (over z, y).
Axes of the slice: x: 2, y: 2, z: 4, core: 2. Of those that a mesh axis runs over, the one named last changes fastest.
Arguments:
- field: float32 [12, 64, 64, 128], P(None, 'gx', 'gy'), may hold values from -16 to 16
- diffusion: float32 [12], replicated, may hold values from 0.02 to 0.15
- prefactor: float32 [12], replicated, may hold values from 0.05 to 0.3
- activation: float32 [12], replicated, may hold values from 0.5 to 2
- mixing: float32 [12, 12], replicated, may hold values from -1.75 to 1.75
- basis_x: float32 [64, 64], P('gx'), may hold values from -1 to 1, as said below
- basis_y: float32 [64, 64], P('gy'), may hold values from -1 to 1, as said below
- basis_z: float32 [128, 32], replicated, may hold values from -1 to 1, as said below
- basis_v: float32 [12, 6], replicated, may hold values from -1 to 1, as said below
Outputs:
- state: float32 [12, 64, 64, 128], P(None, 'gx', 'gy')
- recon: float32 [12, 64, 64, 128], P(None, 'gx', 'gy')
- residual: float32 [12], replicated
Inputs may be any that keep to these rules, and one draw needn't show every extreme that they name: `basis_x`: its 64 columns are mutually orthogonal, each of norm between 0.5 and 1. `basis_y`: its 64 columns are orthonormal. `basis_z`: its 32 columns are orthonormal. `basis_v`: its 6 columns are orthonormal.
All inputs are finite; a program needn't handle non-finite values.
Results may differ from a plain program's by a relative error of at most 0.00013.
Values sent between devices are 32-bit elements; how exact they have to be, the bound alone decides.
No kernel may reach another device: no remote copies, remote signals or barrier semaphores. Data moves between devices by JAX's collectives and lax.ppermute only.
A program may use at most 64 MiB of HBM per device.

v0:
```python
import jax
import jax.numpy as jnp
from jax import lax
from jax.sharding import PartitionSpec as P

HIGH = lax.Precision.HIGHEST


def padded_2(array, sides, width):
    for axis, dim in sides:
        peers, length = (lax.axis_size(axis), array.shape[dim])
        up = [(i, (i + 1) % peers) for i in range(peers - 1)]
        down = [(j, i) for i, j in up]
        last = lax.slice_in_dim(array, length - width, length, axis=dim)
        first = lax.slice_in_dim(array, 0, width, axis=dim)
        before = lax.ppermute(last, axis, up)
        after = lax.ppermute(first, axis, down)
        array = jnp.concatenate([before, array, after], axis=dim)
    return array


def lap_core(padded):
    centre = padded[:, 1:-1, 1:-1, 1:-1]
    summed = padded[:, 2:, 1:-1, 1:-1] + padded[:, :-2, 1:-1, 1:-1]
    summed = summed + padded[:, 1:-1, 2:, 1:-1] + padded[:, 1:-1, :-2, 1:-1]
    summed = summed + padded[:, 1:-1, 1:-1, 2:] + padded[:, 1:-1, 1:-1, :-2]
    return summed - 6.0 * centre


def reaction(centre, coeffs):
    diffusion, prefactor, activation, mixing = coeffs
    temper = 1.5 + jnp.tanh(centre[0])
    rate_terms = (
        prefactor[:, None, None, None]
        * jnp.exp(-activation[:, None, None, None] / temper[None])
        * centre
    )
    return jnp.einsum("vw,wxyz->vxyz", mixing, rate_terms, precision=HIGH)


def tendency(rimmed, centre, coeffs):
    padded = jnp.pad(rimmed, ((0, 0), (0, 0), (0, 0), (1, 1)))
    return coeffs[0][:, None, None, None] * lap_core(padded) + reaction(centre, coeffs)


def inside_mask(rows_x, rows_y):
    pos_x = lax.axis_index("gx") * rows_x + jnp.arange(rows_x + 2) - 1
    pos_y = lax.axis_index("gy") * rows_y + jnp.arange(rows_y + 2) - 1
    in_x = (pos_x >= 0) & (pos_x < rows_x * lax.axis_size("gx"))
    in_y = (pos_y >= 0) & (pos_y < rows_y * lax.axis_size("gy"))
    return in_x[:, None] & in_y[None, :]


def step_deep(state, coeffs, inside):
    wide = padded_2(state, (("gx", 1), ("gy", 2)), 2)
    centre = wide[:, 1:-1, 1:-1]
    section_wide = centre + tendency(wide, centre, coeffs)
    section_wide = jnp.where(inside[None, :, :, None], section_wide, 0.0)
    section = section_wide[:, 1:-1, 1:-1]
    return 0.5 * (state + section + tendency(section_wide, section, coeffs))


def on_device(field, diffusion, prefactor, activation, mixing, basis_x, basis_y, basis_z, basis_v):
    coeffs = (diffusion, prefactor, activation, mixing)
    rows_x = field.shape[1]
    rows_y = field.shape[2]
    state = field
    inside = inside_mask(rows_x, rows_y)
    state = step_deep(state, coeffs, inside)
    rank_z = basis_z.shape[1]
    rank_v = basis_v.shape[1]
    width = rank_z * rank_v
    proj_z = jnp.einsum("vxyz,zr->vxyr", state, basis_z, precision=HIGH)
    packed = jnp.einsum("vxyr,vs->xyrs", proj_z, basis_v, precision=HIGH)
    packed = packed.reshape(rows_x, rows_y, width)
    columns = basis_x
    part_x = lax.psum_scatter(
        jnp.einsum("xa,xyk->ayk", columns, packed, precision=HIGH),
        "gx",
        scatter_dimension=0,
        tiled=True,
    )
    core_block = jnp.einsum("ayk,yb->abk", part_x, basis_y, precision=HIGH)
    core_block = lax.psum(core_block, "gy")
    mixed_y = jnp.einsum("abk,yb->ayk", core_block, basis_y, precision=HIGH)
    columns = basis_x
    decoded = jnp.einsum(
        "xa,ayk->xyk", columns, lax.all_gather(mixed_y, "gx", axis=0, tiled=True), precision=HIGH
    )
    decoded = decoded.reshape(rows_x, rows_y, rank_z, rank_v)
    back_v = jnp.einsum("xyrs,vs->vxyr", decoded, basis_v, precision=HIGH)
    recon = jnp.einsum("vxyr,zr->vxyz", back_v, basis_z, precision=HIGH)
    error = state - recon
    miss_local = jnp.sum(error * error, axis=(1, 2, 3))
    mass_local = jnp.sum(state * state, axis=(1, 2, 3))
    miss, mass = lax.psum((miss_local, mass_local), ("gx", "gy"))
    residual = jnp.sqrt(miss / (mass + 1e-06))
    return (state, recon, residual)


def solution(mesh):
    return jax.shard_map(
        on_device,
        mesh=mesh,
        in_specs=(
            P(None, "gx", "gy", None),
            P(),
            P(),
            P(),
            P(),
            P("gx", None),
            P("gy", None),
            P(),
            P(),
        ),
        out_specs=(P(None, "gx", "gy", None), P(None, "gx", "gy", None), P()),
        check_vma=False,
    )
```

profile of v0, /device:TPU:0, one launch (start us, length us, event | category | flops | bytes accessed | tf_op | source)
XLA Modules:
  0.0 209.1 jit_solution(7740615977400366910)
XLA Ops:
  7.2 0.0 copy-start
  7.2 0.0 copy-start.2
  7.2 0.0 reduce-scatter.2.cloned.1.call-start
  7.2 1.0 fusion.57
  8.3 2.4 %collective-permute-start = (f32[12,2,8,128]{3,0,2,1:T(8,128)S(1)}, f32[12,2,8,128]{3,0,2,1:T(8,128)S(1)}, u32[]{:S(2)}, u32[]{:S(2)}) collective-permute-start(f32[12,2,8,128]{3,0,2,1:T(8,128)S(1)} %copy.76), channel_id=1, source_target_pairs={{0,8},{8,16},{16,24},{1,9},{9,17},{17,25},{2,10},{10,18},{18,26},{... | collective-permute-start | bytes 294920 | tf_op jit(solution)/shard_map/ppermute | solution.py:16
  10.8 1.3 collective-permute-start.1
  12.1 0.0 collective-permute-done
  12.1 0.0 copy-done.2
  12.1 0.0 copy-start.7
  12.1 0.5 copy_dynamic-update-slice_fusion
  12.6 3.5 %collective-permute-done.1 = f32[12,2,8,128]{3,0,2,1:T(8,128)S(1)} collective-permute-done((f32[12,2,8,128]{3,0,2,1:T(8,128)S(1)}, f32[12,2,8,128]{3,0,2,1:T(8,128)S(1)}, u32[]{:S(2)}, u32[]{:S(2)}) %collective-permute-start.1) | collective-permute-done | bytes 98336 | tf_op jit(solution)/shard_map/ppermute | solution.py:17
  16.2 3.4 %collective-permute-start.2 = (f32[12,20,2,128]{3,0,2,1:T(8,128)S(1)}, f32[12,20,2,128]{3,0,2,1:T(8,128)S(1)}, u32[]{:S(2)}, u32[]{:S(2)}) collective-permute-start(f32[12,20,2,128]{3,0,2,1:T(8,128)S(1)} %get-tuple-element.19), channel_id=1, source_target_pairs={{0,1},{1,2},{2,3},{3,4},{4,5},{5,6},{6,7},{8,9},{9,10},{10,11},{11... | collective-permute-start | bytes 737288 | tf_op jit(solution)/shard_map/ppermute | solution.py:16
  19.6 1.3 collective-permute-start.3
  20.9 0.0 copy-done.7
  20.9 0.1 broadcast_and_fusion
  21.0 0.0 copy-start.6
  21.0 0.0 copy-start.8
  21.0 0.0 copy-start.9
  21.0 4.2 %collective-permute-done.2 = f32[12,20,2,128]{3,0,2,1:T(8,128)S(1)} collective-permute-done((f32[12,20,2,128]{3,0,2,1:T(8,128)S(1)}, f32[12,20,2,128]{3,0,2,1:T(8,128)S(1)}, u32[]{:S(2)}, u32[]{:S(2)}) %collective-permute-start.2) | collective-permute-done | bytes 245792 | tf_op jit(solution)/shard_map/ppermute | solution.py:16
  25.2 4.6 %collective-permute-done.3 = f32[12,20,2,128]{3,0,2,1:T(8,128)S(1)} collective-permute-done((f32[12,20,2,128]{3,0,2,1:T(8,128)S(1)}, f32[12,20,2,128]{3,0,2,1:T(8,128)S(1)}, u32[]{:S(2)}, u32[]{:S(2)}) %collective-permute-start.3) | collective-permute-done | bytes 245792 | tf_op jit(solution)/shard_map/ppermute | solution.py:17
  29.8 0.2 pad_maximum_fusion
  30.0 0.1 fusion.41
  30.1 0.0 copy-done.6
  30.1 0.0 copy-done.8
  30.1 0.0 copy-done.9
  30.1 2.3 %fusion.8 = f32[12,18,10,128]{3,0,2,1:T(8,128)S(1)} fusion(f32[12,20,12,128]{3,0,2,1:T(8,128)S(1)} %pad_maximum_fusion, f32[12,20,8,128]{3,0,2,1:T(8,128)S(1)} %constant_dynamic-update-slice_fusion, f32[12,20,2,128]{3,0,2,1:T(8,128)S(1)} %collective-permute-done.2, f32[12,20,2,128]{3,0,2,1:T(8,128)S(1)} %collective-permute-done.3, ...), kind=kOutput, calls=%fused_computation.14 | convolution fusion | flops 44236800 | bytes 11096576 | tf_op jit(solution)/shard_map/vw,wxyz->vxyz/dot_general | solution.py:38
  32.5 0.1 fusion.42
  32.6 2.2 %fusion.23 = f32[12,16,8,128]{3,0,2,1:T(8,128)S(1)} fusion(f32[12,18,10,128]{3,0,2,1:T(8,128)S(1)} %fusion.8, f32[16,8,128]{2,1,0:T(8,128)S(1)} %bitcast.62, f32[12]{0:T(128)S(1)} %neg.5, f32[12]{0:T(128)S(1)} %copy-done.8, f32[12]{0:T(128)S(1)} %copy-done.9, f32[12,16,8,128]{3,2,1,0:T(8,128)S(1)} %copy-done.2, f32[12,12]{1,0:T(8,128)S(1)} %copy-done.6), kind=kOutput, calls=%fused_computation.37 | convolution fusion | flops 31260672 | bytes 9414144 | tf_op jit(solution)/shard_map/vw,wxyz->vxyz/dot_general | solution.py:38
  34.8 0.0 copy-done
  34.8 0.0 copy-start.5
  34.8 1.0 fusion.44
  35.8 0.0 copy-done.5
  35.8 0.0 copy-start.3
  35.8 0.7 fusion.51
  36.5 0.5 copy.49
  37.1 0.0 copy-start.4
  37.1 0.0 copy-done.3
  37.1 1.7 convolution_bitcast_fusion.3
  38.7 1.1 copy.51
  39.8 0.0 reduce-scatter.2.cloned.1.call-update
  39.9 0.0 all-reduce.5.cloned.1.call-start
  39.9 27.8 %reduce-scatter.2.cloned.1.call-done = f32[16,8,192]{2,1,0:T(8,128)} async-done(((f32[64,8,192]{2,1,0:T(8,128)}), f32[16,8,192]{2,1,0:T(8,128)}) %reduce-scatter.2.cloned.1.call-update) | async-done | bytes 98320 | tf_op jit(solution)/shard_map/reduce_scatter | solution.py:77
  67.7 0.0 copy-done.4
  67.7 2.9 %convolution_bitcast_fusion.1 = f32[16,64,192]{2,1,0:T(8,128)} fusion(f32[16,8,192]{2,1,0:T(8,128)} %reduce-scatter.2.cloned.1.call-done, f32[8,64]{1,0:T(8,128)S(1)} %copy-done.4), kind=kOutput, calls=%fused_computation.23 | convolution fusion | flops 18874368 | bytes 886784 | tf_op jit(solution)/shard_map/ayk,yb->abk/dot_general | solution.py:83
  70.6 0.0 all-reduce.5.cloned.1.call-update
  70.6 1.1 copy.57
  71.7 77.8 %all-reduce.5.cloned.1.call-done = f32[16,64,192]{2,1,0:T(8,128)} async-done(((f32[16,64,192]{2,1,0:T(8,128)}), f32[16,64,192]{2,1,0:T(8,128)}) %all-reduce.5.cloned.1.call-update) | async-done | bytes 786448 | tf_op jit(solution)/shard_map/psum | solution.py:84
  149.5 1.9 convolution_bitcast_fusion.5
  151.3 7.3 %all_gather.3 = f32[64,8,192]{2,1,0:T(8,128)S(1)} all-gather(f32[16,8,192]{2,1,0:T(8,128)S(1)} %convolution_bitcast_fusion.5), channel_id=1, replica_groups=mesh['gx'=4,'gy'=8] {'gx'}, dimensions={0}, use_global_device_ids=true | all-gather | bytes 491520 | tf_op jit(solution)/shard_map/all_gather | solution.py:88
  158.7 0.5 convolution_bitcast_fusion.4
  159.2 0.3 copy.53
  159.5 0.6 copy.54
  160.1 1.0 convolution_bitcast_fusion
  161.2 0.9 fusion.31
  162.1 0.0 copy-start.1
  162.1 0.7 multiply_reduce_fusion
  162.8 38.9 %all-reduce.2 = (f32[12]{0:T(128)S(1)}, f32[12]{0:T(128)S(1)}) all-reduce(f32[12]{0:T(128)S(1)} %get-tuple-element.16, f32[12]{0:T(128)S(1)} %get-tuple-element.15), channel_id=1, replica_groups=mesh['gx'=4,'gy'=8] {'gx','gy'}, use_global_device_ids=true, to_apply=%region_3.4 | all-reduce | flops 24 | bytes 192 | tf_op jit(solution)/shard_map/psum | solution.py:96
  201.7 0.5 fusion.55
  202.2 0.0 copy-done.1
  (9 shorter events, 0.2 us)
Async XLA Ops:
  7.2 27.6 %copy-start = (f32[128,32]{0,1:T(8,128)S(1)}, f32[128,32]{0,1:T(8,128)}, u32[]{:S(2)}) copy-start(f32[128,32]{0,1:T(8,128)} %param.16) | copy-start | bytes 49156
  7.2 4.9 %copy-start.2 = (f32[12,16,8,128]{3,2,1,0:T(8,128)S(1)}, f32[12,16,8,128]{3,2,1,0:T(8,128)}, u32[]{:S(2)}) copy-start(f32[12,16,8,128]{3,2,1,0:T(8,128)} %param.9) | copy-start | bytes 2359300
  7.2 60.5 %reduce-scatter.2.cloned.1.call-start = ((), (), s32[]{:S(2)}) async-start(), calls=%async_computation.1 | async-start | bytes 655360 | tf_op jit(solution)/shard_map/reduce_scatter | solution.py:77
  8.3 3.8 %collective-permute-start = (f32[12,2,8,128]{3,0,2,1:T(8,128)S(1)}, f32[12,2,8,128]{3,0,2,1:T(8,128)S(1)}, u32[]{:S(2)}, u32[]{:S(2)}) collective-permute-start(f32[12,2,8,128]{3,0,2,1:T(8,128)S(1)} %copy.76), channel_id=1, source_target_pairs={{0,8},{8,16},{16,24},{1,9},{9,17},{17,25},{2,10},{10,18},{18,26},{... | collective-permute-start | bytes 294920 | tf_op jit(solution)/shard_map/ppermute | solution.py:16
  10.8 5.3 %collective-permute-start.1 = (f32[12,2,8,128]{3,0,2,1:T(8,128)S(1)}, f32[12,2,8,128]{3,0,2,1:T(8,128)S(1)}, u32[]{:S(2)}, u32[]{:S(2)}) collective-permute-start(f32[12,2,8,128]{3,0,2,1:T(8,128)S(1)} %copy.77), channel_id=1, source_target_pairs={{8,0},{16,8},{24,16},{9,1},{17,9},{25,17},{10,2},{18,10},{26,18},{... | collective-permute-start | bytes 294920 | tf_op jit(solution)/shard_map/ppermute | solution.py:17
  12.1 8.8 %copy-start.7 = (f32[12]{0:T(128)S(1)}, f32[12]{0:T(128)}, u32[]{:S(2)}) copy-start(f32[12]{0:T(128)} %param.12) | copy-start | bytes 148
  16.2 9.0 %collective-permute-start.2 = (f32[12,20,2,128]{3,0,2,1:T(8,128)S(1)}, f32[12,20,2,128]{3,0,2,1:T(8,128)S(1)}, u32[]{:S(2)}, u32[]{:S(2)}) collective-permute-start(f32[12,20,2,128]{3,0,2,1:T(8,128)S(1)} %get-tuple-element.19), channel_id=1, source_target_pairs={{0,1},{1,2},{2,3},{3,4},{4,5},{5,6},{6,7},{8,9},{9,10},{10,11},{11... | collective-permute-start | bytes 737288 | tf_op jit(solution)/shard_map/ppermute | solution.py:16
  19.6 10.2 %collective-permute-start.3 = (f32[12,20,2,128]{3,0,2,1:T(8,128)S(1)}, f32[12,20,2,128]{3,0,2,1:T(8,128)S(1)}, u32[]{:S(2)}, u32[]{:S(2)}) collective-permute-start(f32[12,20,2,128]{3,0,2,1:T(8,128)S(1)} %get-tuple-element.20), channel_id=1, source_target_pairs={{1,0},{2,1},{3,2},{4,3},{5,4},{6,5},{7,6},{9,8},{10,9},{11,10},{12... | collective-permute-start | bytes 737288 | tf_op jit(solution)/shard_map/ppermute | solution.py:17
  21.0 9.1 %copy-start.6 = (f32[12,12]{1,0:T(8,128)S(1)}, f32[12,12]{1,0:T(8,128)}, u32[]{:S(2)}) copy-start(f32[12,12]{1,0:T(8,128)} %param.13) | copy-start | bytes 1732
  21.0 9.1 %copy-start.8 = (f32[12]{0:T(128)S(1)}, f32[12]{0:T(128)}, u32[]{:S(2)}) copy-start(f32[12]{0:T(128)} %param.11) | copy-start | bytes 148
  21.0 9.1 %copy-start.9 = (f32[12]{0:T(128)S(1)}, f32[12]{0:T(128)}, u32[]{:S(2)}) copy-start(f32[12]{0:T(128)} %param.10) | copy-start | bytes 148
  34.8 1.0 copy-start.5
  35.8 1.3 copy-start.3
  37.1 30.6 %copy-start.4 = (f32[8,64]{1,0:T(8,128)S(1)}, f32[8,64]{1,0:T(8,128)}, u32[]{:S(2)}) copy-start(f32[8,64]{1,0:T(8,128)} %param.15) | copy-start | bytes 6148
  39.9 109.6 %all-reduce.5.cloned.1.call-start = ((), (), s32[]{:S(2)}) async-start(), calls=%async_computation.2 | async-start | bytes 2097152 | tf_op jit(solution)/shard_map/psum | solution.py:84
  162.1 40.1 %copy-start.1 = (f32[12,16,8,128]{3,2,1,0:T(8,128)}, f32[12,16,8,128]{3,2,1,0:T(8,128)S(1)}, u32[]{:S(2)}) copy-start(f32[12,16,8,128]{3,2,1,0:T(8,128)S(1)} %fusion.31) | copy-start | bytes 2359300
Sparse Core Ops, SparseCore 0:
  40.0 27.6 reduce-scatter.1
  71.2 78.2 all-reduce.4
where the time goes:
time: 209 us
  waiting for transfers between devices  118 us (56%)
  blocking collectives  46.3 us (22%)
  matrix products  15.1 us (7%)
  between operations  14.4 us (7%)
  starting transfers between devices  8.51 us (4%)
  local copies, waits for them, and re-layouts  5.35 us (3%)
    psum x1, waiting for transfers between devices, on_device(): core_block = lax.psum(core_block, 'gy')  77.8 us
    psum x1, blocking collectives, on_device(): miss, mass = lax.psum((miss_local, mass_local), ('gx', 'gy'))  38.9 us
    reduce_scatter x1, waiting for transfers between devices, on_device(): lax.psum_scatter(jnp.einsum('xa,xyk->ayk', columns, packed, precision=HIG...  27.8 us
    ppermute x2, waiting for transfers between devices, padded_2(): after = lax.ppermute(first, axis, down)  8.07 us
    all_gather x1, blocking collectives, on_device(): lax.all_gather(mixed_y, 'gx', axis=0, tiled=True)  7.32 us
    ppermute x2, starting transfers between devices, padded_2(): before = lax.ppermute(last, axis, up)  5.85 us
    dot_general x2, matrix products, reaction(): return jnp.einsum('vw,wxyz->vxyz', mixing, rate_terms, precision=HIGH)  4.55 us
  transfers between devices with their start and end apart: 6, of which 5 were waited for; matrix products, arithmetic and copies ran while one was open for 1% of the time, Pallas kernels for 0%

commit v1 on v0

--- a/solution.py
+++ b/solution.py
@@ -81,7 +81,7 @@
         tiled=True,
     )
     core_block = jnp.einsum("ayk,yb->abk", part_x, basis_y, precision=HIGH)
-    core_block = lax.psum(core_block, "gy")
+    core_block = jnp.sum(lax.all_gather(core_block, "gy"), axis=0)
     mixed_y = jnp.einsum("abk,yb->ayk", core_block, basis_y, precision=HIGH)
     columns = basis_x
     decoded = jnp.einsum(

time: 209 us -> 258 us (1.23)
  waiting for transfers between devices: 118 us -> 164 us
  other arithmetic: 1.65 us -> 6.03 us
    all_gather x0 -> x1, waiting for transfers between devices: none -> 124 us  [on_device(): core_block = jnp.sum(lax.all_gather(core_block, 'gy'), axis=0)]
    psum x1 -> x0, waiting for transfers between devices: 77.8 us -> none  [on_device(): core_block = lax.psum(core_block, 'gy')]
    reduce_sum x0 -> x1, other arithmetic: none -> 4.38 us  [on_device(): core_block = jnp.sum(lax.all_gather(core_block, 'gy'), axis=0)]
where the time goes in v1:
time: 258 us; the launch traced here: 257 us
  waiting for transfers between devices  164 us (64%)
  blocking collectives  45.7 us (18%)
  matrix products  14.8 us (6%)
  between operations  14.4 us (6%)
  starting transfers between devices  8.51 us (3%)
  other arithmetic  6.03 us (2%)
  local copies, waits for them, and re-layouts  4.25 us (2%)
    all_gather x1, waiting for transfers between devices, on_device(): core_block = jnp.sum(lax.all_gather(core_block, 'gy'), axis=0)  124 us
    psum x1, blocking collectives, on_device(): miss, mass = lax.psum((miss_local, mass_local), ('gx', 'gy'))  38.4 us
    reduce_scatter x1, waiting for transfers between devices, on_device(): lax.psum_scatter(jnp.einsum('xa,xyk->ayk', columns, packed, precision=HIG...  27.8 us
    ppermute x2, waiting for transfers between devices, padded_2(): after = lax.ppermute(first, axis, down)  8.07 us
    all_gather x1, blocking collectives, on_device(): lax.all_gather(mixed_y, 'gx', axis=0, tiled=True)  7.32 us
    ppermute x2, starting transfers between devices, padded_2(): before = lax.ppermute(last, axis, up)  5.85 us
  transfers between devices with their start and end apart: 6, of which 5 were waited for; matrix products, arithmetic and copies ran while one was open for 1% of the time, Pallas kernels for 0%

profile of v1, /device:TPU:0, one launch (start us, length us, event | category | flops | bytes accessed | tf_op | source)
XLA Modules:
  0.0 257.2 jit_solution(7537983616450086570)
XLA Ops:
  7.2 0.0 copy-start
  7.2 0.0 copy-start.2
  7.2 0.0 reduce-scatter.2.cloned.1.call-start
  7.2 1.0 fusion.58
  8.3 2.4 collective-permute-start
  10.8 1.3 collective-permute-start.1
  12.1 0.0 collective-permute-done
  12.1 0.0 copy-done.2
  12.1 0.0 copy-start.7
  12.1 0.5 copy_dynamic-update-slice_fusion
  12.6 3.5 %collective-permute-done.1 = f32[12,2,8,128]{3,0,2,1:T(8,128)S(1)} collective-permute-done((f32[12,2,8,128]{3,0,2,1:T(8,128)S(1)}, f32[12,2,8,128]{3,0,2,1:T(8,128)S(1)}, u32[]{:S(2)}, u32[]{:S(2)}) %collective-permute-start.1) | collective-permute-done | bytes 98336 | tf_op jit(solution)/shard_map/ppermute | solution.py:17
  16.2 3.4 %collective-permute-start.2 = (f32[12,20,2,128]{3,0,2,1:T(8,128)S(1)}, f32[12,20,2,128]{3,0,2,1:T(8,128)S(1)}, u32[]{:S(2)}, u32[]{:S(2)}) collective-permute-start(f32[12,20,2,128]{3,0,2,1:T(8,128)S(1)} %get-tuple-element.19), channel_id=1, source_target_pairs={{0,1},{1,2},{2,3},{3,4},{4,5},{5,6},{6,7},{8,9},{9,10},{10,11},{11... | collective-permute-start | bytes 737288 | tf_op jit(solution)/shard_map/ppermute | solution.py:16
  19.6 1.3 collective-permute-start.3
  20.9 0.0 copy-done.7
  20.9 0.1 broadcast_and_fusion
  21.0 0.0 copy-start.6
  21.0 0.0 copy-start.8
  21.0 0.0 copy-start.9
  21.0 4.2 %collective-permute-done.2 = f32[12,20,2,128]{3,0,2,1:T(8,128)S(1)} collective-permute-done((f32[12,20,2,128]{3,0,2,1:T(8,128)S(1)}, f32[12,20,2,128]{3,0,2,1:T(8,128)S(1)}, u32[]{:S(2)}, u32[]{:S(2)}) %collective-permute-start.2) | collective-permute-done | bytes 245792 | tf_op jit(solution)/shard_map/ppermute | solution.py:16
  25.2 4.6 %collective-permute-done.3 = f32[12,20,2,128]{3,0,2,1:T(8,128)S(1)} collective-permute-done((f32[12,20,2,128]{3,0,2,1:T(8,128)S(1)}, f32[12,20,2,128]{3,0,2,1:T(8,128)S(1)}, u32[]{:S(2)}, u32[]{:S(2)}) %collective-permute-start.3) | collective-permute-done | bytes 245792 | tf_op jit(solution)/shard_map/ppermute | solution.py:17
  29.8 0.2 pad_maximum_fusion
  30.0 0.1 fusion.42
  30.1 0.0 copy-done.6
  30.1 0.0 copy-done.8
  30.1 0.0 copy-done.9
  30.1 2.3 fusion.8
  32.5 0.1 fusion.43
  32.6 2.2 fusion.23
  34.8 0.0 copy-done
  34.8 0.0 copy-start.5
  34.8 1.0 fusion.45
  35.8 0.0 copy-done.5
  35.8 0.0 copy-start.3
  35.8 0.7 fusion.52
  36.5 0.0 copy-start.4
  36.6 0.5 copy.49
  37.1 0.0 copy-done.3
  37.1 2.4 convolution_bitcast_fusion.3
  39.5 0.0 reduce-scatter.2.cloned.1.call-update
  39.6 0.0 all-gather.3.cloned.1.call-start
  39.6 27.8 %reduce-scatter.2.cloned.1.call-done = f32[16,8,192]{2,0,1:T(8,128)} async-done(((f32[64,8,192]{2,0,1:T(8,128)}), f32[16,8,192]{2,0,1:T(8,128)}) %reduce-scatter.2.cloned.1.call-update) | async-done | bytes 98320 | tf_op jit(solution)/shard_map/reduce_scatter | solution.py:77
  67.4 0.0 copy-done.4
  67.4 3.0 %convolution_bitcast_fusion.1 = f32[16,64,192]{2,1,0:T(8,128)} fusion(f32[16,8,192]{2,0,1:T(8,128)} %reduce-scatter.2.cloned.1.call-done, f32[8,64]{1,0:T(8,128)S(1)} %copy-done.4), kind=kOutput, calls=%fused_computation.23 | convolution fusion | flops 18874368 | bytes 886784 | tf_op jit(solution)/shard_map/ayk,yb->abk/dot_general | solution.py:83
  70.3 0.0 all-gather.3.cloned.1.call-update
  70.4 1.1 copy.57
  71.5 123.5 %all-gather.3.cloned.1.call-done = f32[128,64,192]{2,1,0:T(8,128)} async-done(((f32[16,64,192]{2,1,0:T(8,128)}), f32[128,64,192]{2,1,0:T(8,128)}) %all-gather.3.cloned.1.call-update) | async-done | bytes 6291472 | tf_op jit(solution)/shard_map/all_gather | solution.py:84
  195.0 4.4 %reduce_sum.27 = f32[16,64,192]{2,1,0:T(8,128)S(1)} reduce(f32[8,16,64,192]{3,2,1,0:T(8,128)} %bitcast.59, f32[]{:T(128)} %constant.6.clone.1), dimensions={0}, to_apply=%region_1.2 | reduce | flops 1376256 | bytes 7077892 | tf_op jit(solution)/shard_map/reduce_sum | solution.py:84
  199.4 0.7 convolution_bitcast_fusion.5
  200.0 7.3 %all_gather.11 = f32[64,8,192]{2,1,0:T(8,128)S(1)} all-gather(f32[16,8,192]{2,1,0:T(8,128)S(1)} %convolution_bitcast_fusion.5), channel_id=1, replica_groups=mesh['gx'=4,'gy'=8] {'gx'}, dimensions={0}, use_global_device_ids=true | all-gather | bytes 491520 | tf_op jit(solution)/shard_map/all_gather | solution.py:88
  207.3 0.5 convolution_bitcast_fusion.4
  207.9 0.3 copy.53
  208.2 0.6 copy.54
  208.8 1.0 convolution_bitcast_fusion
  209.8 0.9 fusion.31
  210.8 0.0 copy-start.1
  210.8 0.7 multiply_reduce_fusion
  211.5 38.4 %all-reduce.2 = (f32[12]{0:T(128)S(1)}, f32[12]{0:T(128)S(1)}) all-reduce(f32[12]{0:T(128)S(1)} %get-tuple-element.16, f32[12]{0:T(128)S(1)} %get-tuple-element.15), channel_id=1, replica_groups=mesh['gx'=4,'gy'=8] {'gx','gy'}, use_global_device_ids=true, to_apply=%region_3.4 | all-reduce | flops 24 | bytes 192 | tf_op jit(solution)/shard_map/psum | solution.py:96
  249.8 0.5 fusion.56
  250.4 0.0 copy-done.1
  (9 shorter events, 0.2 us)
Async XLA Ops:
  7.2 27.6 %copy-start = (f32[128,32]{0,1:T(8,128)S(1)}, f32[128,32]{0,1:T(8,128)}, u32[]{:S(2)}) copy-start(f32[128,32]{0,1:T(8,128)} %param.16) | copy-start | bytes 49156
  7.2 4.9 %copy-start.2 = (f32[12,16,8,128]{3,2,1,0:T(8,128)S(1)}, f32[12,16,8,128]{3,2,1,0:T(8,128)}, u32[]{:S(2)}) copy-start(f32[12,16,8,128]{3,2,1,0:T(8,128)} %param.9) | copy-start | bytes 2359300
  7.2 60.2 %reduce-scatter.2.cloned.1.call-start = ((), (), s32[]{:S(2)}) async-start(), calls=%async_computation.1 | async-start | bytes 655360 | tf_op jit(solution)/shard_map/reduce_scatter | solution.py:77
  8.3 3.8 %collective-permute-start = (f32[12,2,8,128]{3,0,2,1:T(8,128)S(1)}, f32[12,2,8,128]{3,0,2,1:T(8,128)S(1)}, u32[]{:S(2)}, u32[]{:S(2)}) collective-permute-start(f32[12,2,8,128]{3,0,2,1:T(8,128)S(1)} %copy.78), channel_id=1, source_target_pairs={{0,8},{8,16},{16,24},{1,9},{9,17},{17,25},{2,10},{10,18},{18,26},{... | collective-permute-start | bytes 294920 | tf_op jit(solution)/shard_map/ppermute | solution.py:16
  10.8 5.3 %collective-permute-start.1 = (f32[12,2,8,128]{3,0,2,1:T(8,128)S(1)}, f32[12,2,8,128]{3,0,2,1:T(8,128)S(1)}, u32[]{:S(2)}, u32[]{:S(2)}) collective-permute-start(f32[12,2,8,128]{3,0,2,1:T(8,128)S(1)} %copy.79), channel_id=1, source_target_pairs={{8,0},{16,8},{24,16},{9,1},{17,9},{25,17},{10,2},{18,10},{26,18},{... | collective-permute-start | bytes 294920 | tf_op jit(solution)/shard_map/ppermute | solution.py:17
  12.1 8.8 %copy-start.7 = (f32[12]{0:T(128)S(1)}, f32[12]{0:T(128)}, u32[]{:S(2)}) copy-start(f32[12]{0:T(128)} %param.12) | copy-start | bytes 148
  16.2 9.0 %collective-permute-start.2 = (f32[12,20,2,128]{3,0,2,1:T(8,128)S(1)}, f32[12,20,2,128]{3,0,2,1:T(8,128)S(1)}, u32[]{:S(2)}, u32[]{:S(2)}) collective-permute-start(f32[12,20,2,128]{3,0,2,1:T(8,128)S(1)} %get-tuple-element.19), channel_id=1, source_target_pairs={{0,1},{1,2},{2,3},{3,4},{4,5},{5,6},{6,7},{8,9},{9,10},{10,11},{11... | collective-permute-start | bytes 737288 | tf_op jit(solution)/shard_map/ppermute | solution.py:16
  19.6 10.2 %collective-permute-start.3 = (f32[12,20,2,128]{3,0,2,1:T(8,128)S(1)}, f32[12,20,2,128]{3,0,2,1:T(8,128)S(1)}, u32[]{:S(2)}, u32[]{:S(2)}) collective-permute-start(f32[12,20,2,128]{3,0,2,1:T(8,128)S(1)} %get-tuple-element.20), channel_id=1, source_target_pairs={{1,0},{2,1},{3,2},{4,3},{5,4},{6,5},{7,6},{9,8},{10,9},{11,10},{12... | collective-permute-start | bytes 737288 | tf_op jit(solution)/shard_map/ppermute | solution.py:17
  21.0 9.1 %copy-start.6 = (f32[12,12]{1,0:T(8,128)S(1)}, f32[12,12]{1,0:T(8,128)}, u32[]{:S(2)}) copy-start(f32[12,12]{1,0:T(8,128)} %param.13) | copy-start | bytes 1732
  21.0 9.1 %copy-start.8 = (f32[12]{0:T(128)S(1)}, f32[12]{0:T(128)}, u32[]{:S(2)}) copy-start(f32[12]{0:T(128)} %param.11) | copy-start | bytes 148
  21.0 9.1 %copy-start.9 = (f32[12]{0:T(128)S(1)}, f32[12]{0:T(128)}, u32[]{:S(2)}) copy-start(f32[12]{0:T(128)} %param.10) | copy-start | bytes 148
  34.8 1.0 copy-start.5
  35.8 1.3 copy-start.3
  36.5 30.8 %copy-start.4 = (f32[8,64]{1,0:T(8,128)S(1)}, f32[8,64]{1,0:T(8,128)}, u32[]{:S(2)}) copy-start(f32[8,64]{1,0:T(8,128)} %param.15) | copy-start | bytes 6148
  39.6 155.4 %all-gather.3.cloned.1.call-start = ((), (), s32[]{:S(2)}) async-start(), calls=%async_computation.2 | async-start | bytes 9437184 | tf_op jit(solution)/shard_map/all_gather | solution.py:84
  210.8 39.6 %copy-start.1 = (f32[12,16,8,128]{3,2,1,0:T(8,128)}, f32[12,16,8,128]{3,2,1,0:T(8,128)S(1)}, u32[]{:S(2)}) copy-start(f32[12,16,8,128]{3,2,1,0:T(8,128)S(1)} %fusion.31) | copy-start | bytes 2359300
Sparse Core Ops, SparseCore 0:
  39.7 27.6 reduce-scatter.1
  70.5 124.4 all-gather.2
